TPU v7x, 32 devices: a whole 2x2x4 slice. The times are simulated.
32 devices in a mesh: ffn: 16 (over z, y, core), tok: 2 (over x).
Axes of the slice: x: 2, y: 2, z: 4, core: 2. Of those that a mesh axis runs over, the one named last changes fastest.
Arguments:
- tokens: bfloat16 [16384, 768], P(('ffn', 'tok')), may hold values from -6 to 6
- joint_proj: bfloat16 [768, 2304], replicated, may hold values from -0.21875 to 0.21875
- query_bias: bfloat16 [768], replicated, may hold values from -1.5 to 1.5
- value_bias: bfloat16 [768], replicated, may hold values from -1.5 to 1.5
- out_proj: bfloat16 [768, 768], replicated, may hold values from -1.75 to 1.75
- out_bias: bfloat16 [768], replicated, may hold values from -1.5 to 1.5
- first_gain: float32 [768], replicated, may hold values from 0.5 to 1.5
- first_shift: float32 [768], replicated, may hold values from -1.5 to 1.5
- inner_proj: bfloat16 [768, 3072], P(None, 'ffn'), may hold values from -0.21875 to 0.21875
- inner_bias: bfloat16 [3072], P('ffn'), may hold values from -1.5 to 1.5
- outer_proj: bfloat16 [3072, 768], P('ffn'), may hold values from -0.15625 to 0.15625
- outer_bias: bfloat16 [768], replicated, may hold values from -1.5 to 1.5
- second_gain: float32 [768], replicated, may hold values from 0.5 to 1.5
- second_shift: float32 [768], replicated, may hold values from -1.5 to 1.5
- segment_ids: int32 [16384], P(('ffn', 'tok')), may hold values from 0 to 3, as said below
- cls_positions: int32 [32, 4], P(('ffn', 'tok')), may hold values from 0 to 480, as said below
- widths: int32 [2, 2], replicated, may hold values from 3 to 3072, as said below
- out_grad: bfloat16 [16384, 768], P(('ffn', 'tok')), may hold values from -6 to 6
Outputs:
- output: bfloat16 [16384, 768], P(('ffn', 'tok'))
- cls_states: float32 [32, 4, 768], P(('ffn', 'tok'))
- input_grad: float32 [16384, 768], P(('ffn', 'tok'))
- joint_proj_grad: float32 [768, 2304], replicated
- query_bias_grad: float32 [768], replicated
- value_bias_grad: float32 [768], replicated
- out_proj_grad: float32 [768, 768], replicated
- out_bias_grad: float32 [768], replicated
- first_gain_grad: float32 [768], replicated
- first_shift_grad: float32 [768], replicated
- inner_proj_grad: float32 [768, 3072], P(None, 'ffn')
- inner_bias_grad: float32 [3072], P('ffn')
- outer_proj_grad: float32 [3072, 768], P('ffn')
- outer_bias_grad: float32 [768], replicated
- second_gain_grad: float32 [768], replicated
- second_shift_grad: float32 [768], replicated
Inputs may be any that keep to these rules, and one draw needn't show every extreme that they name: `segment_ids`: each row of 512 tokens holds exactly 4 examples numbered 0 to 3 in order, each of one token or more. `cls_positions`: the first position of each example of a row, counted from the row's start, in the order of the examples; the first is 0; the last example's start reaches the most in some row. `widths`: row m: neurons kept (a multiple of 768, at least 768) and heads kept (a multiple of 3, at least 3) of micro-batch m; one micro-batch keeps all 3072 neurons and all 12 heads.
All inputs are finite; a program needn't handle non-finite values.
Results may differ from a plain program's by a relative error of at most 0.014.
The roundings to bfloat16 on the way count: a program that leaves them out, or rounds other values in their place, can miss the bound.
Values may be sent and summed in bfloat16 or wider, within the bound.
A program may use at most 256 MiB of HBM per device.

v0:
```python
import math
import jax
import jax.numpy as jnp
from jax import lax
from jax.sharding import PartitionSpec as P

HEADS = 12
DH = 64
MB = 2


def normalize(inputs, gain_vec, shift_vec):
    row_mean = jnp.mean(inputs, axis=-1, keepdims=True)
    centred = inputs - row_mean
    row_scale = lax.rsqrt(jnp.mean(centred * centred, axis=-1, keepdims=True) + 1e-12)
    normed = centred * row_scale
    return (normed * gain_vec + shift_vec, normed, row_scale)


def normalize_back(incoming, normed, row_scale, gain_vec):
    gain_grad = jnp.sum(incoming * normed, axis=0)
    shift_grad = jnp.sum(incoming, axis=0)
    scaled_grad = incoming * gain_vec
    inputs_grad = row_scale * (
        scaled_grad
        - jnp.mean(scaled_grad, axis=-1, keepdims=True)
        - normed * jnp.mean(scaled_grad * normed, axis=-1, keepdims=True)
    )
    return (inputs_grad, gain_grad, shift_grad)


def gelu_slope(inputs):
    return (
        0.5 * (1.0 + lax.erf(inputs * 0.7071067811865476))
        + inputs * jnp.exp(-0.5 * inputs * inputs) * 0.3989422804014327
    )


def contract_rows(left_side, right_side):
    return lax.dot_general(
        left_side, right_side, (((0,), (0,)), ((), ())), preferred_element_type=jnp.float32
    )


def contract_cols(left_side, right_side):
    return lax.dot_general(
        left_side, right_side, (((1,), (1,)), ((), ())), preferred_element_type=jnp.float32
    )


def on_device(
    tokens,
    joint_proj,
    query_bias,
    value_bias,
    out_proj,
    out_bias,
    first_gain,
    first_shift,
    inner_proj,
    inner_bias,
    outer_proj,
    outer_bias,
    second_gain,
    second_shift,
    segment_ids,
    cls_positions,
    widths,
    out_grad,
):
    tok_rows, model_width = tokens.shape
    seq_rows = cls_positions.shape[0]
    seq_len = tok_rows // seq_rows
    unit_share = inner_proj.shape[1]
    ffn_count = lax.axis_size("ffn")
    tok_count = lax.axis_size("tok")
    ffn_place = lax.axis_index("ffn")
    tok_place = lax.axis_index("tok")
    per_group = seq_rows * ffn_count * tok_count // MB
    batches = jnp.arange(MB, dtype=jnp.int32)
    own_group = (ffn_place * tok_count + tok_place) * seq_rows // per_group
    own_pick = (batches == own_group).astype(jnp.int32)
    heads_kept = jnp.sum(own_pick * widths[:, 1])
    head_on = (jnp.arange(HEADS, dtype=jnp.int32) < heads_kept).astype(jnp.float32)
    factor = 1.0 / math.sqrt(DH)
    zero_bias = jnp.zeros((model_width,), jnp.bfloat16)
    joint_bias = jnp.concatenate([query_bias, zero_bias, value_bias])
    joint_low = (
        jnp.dot(tokens, joint_proj, preferred_element_type=jnp.float32) + joint_bias
    ).astype(jnp.bfloat16)
    joint_low = joint_low.reshape(seq_rows, seq_len, 3, HEADS, DH)
    queries = joint_low[:, :, 0]
    key_heads = joint_low[:, :, 1]
    value_heads = joint_low[:, :, 2]
    segments = segment_ids.reshape(seq_rows, seq_len)
    same_doc = (segments[:, :, None] == segments[:, None, :])[:, None]

    def scores_of(query_rows, key_rows):
        raw_scores = (
            jnp.einsum("rqhd,rkhd->rhqk", query_rows, key_rows, preferred_element_type=jnp.float32)
            * factor
        )
        return jnp.where(same_doc, raw_scores, -1e30)

    scores = scores_of(queries, key_heads)
    row_peak = jnp.max(scores, axis=-1, keepdims=True)
    log_total = row_peak + jnp.log(jnp.sum(jnp.exp(scores - row_peak), axis=-1, keepdims=True))
    probs_low = jnp.exp(scores - log_total).astype(jnp.bfloat16)
    context = (
        jnp.einsum("rhqk,rkhd->rqhd", probs_low, value_heads, preferred_element_type=jnp.float32)
        * head_on[:, None]
    )
    context_low = context.astype(jnp.bfloat16).reshape(tok_rows, model_width)
    attn_out = jnp.dot(context_low, out_proj, preferred_element_type=jnp.float32) + out_bias
    first_out, first_normed, first_scale = normalize(
        tokens.astype(jnp.float32) + attn_out, first_gain, first_shift
    )
    first_low = first_out.astype(jnp.bfloat16)
    unit_total = unit_share * ffn_count
    stacked = lax.all_gather(jnp.stack([inner_proj.T, outer_proj]), "ffn", axis=1, tiled=True)
    inner_rows, outer_rows = (stacked[0], stacked[1])
    inner_bias_all = lax.all_gather(inner_bias, "ffn", axis=0, tiled=True)
    own_kept = jnp.sum(own_pick * widths[:, 0])
    neuron_on = (jnp.arange(unit_total, dtype=jnp.int32) < own_kept).astype(jnp.float32)
    pre_act = contract_cols(first_low, inner_rows) + inner_bias_all
    act_low = (jax.nn.gelu(pre_act, approximate=False) * neuron_on).astype(jnp.bfloat16)
    ffn_out = jnp.dot(act_low, outer_rows, preferred_element_type=jnp.float32) + outer_bias
    second_out, second_normed, second_scale = normalize(
        first_out + ffn_out, second_gain, second_shift
    )
    output = second_out.astype(jnp.bfloat16)
    cls_states = jnp.take_along_axis(
        second_out.reshape(seq_rows, seq_len, model_width), cls_positions[:, :, None], axis=1
    )
    sum_grad, second_gain_grad, second_shift_grad = normalize_back(
        out_grad.astype(jnp.float32), second_normed, second_scale, second_gain
    )
    ffn_grad = sum_grad.astype(jnp.bfloat16)
    outer_bias_grad = jnp.sum(ffn_grad.astype(jnp.float32), axis=0)
    outer_proj_grad = contract_rows(act_low, ffn_grad)
    act_grad = contract_cols(ffn_grad, outer_rows)
    pre_grad = (act_grad * (gelu_slope(pre_act) * neuron_on)).astype(jnp.bfloat16)
    inner_bias_sum = jnp.sum(pre_grad.astype(jnp.float32), axis=0)
    inner_rows_grad = contract_rows(pre_grad, first_low)
    first_back = jnp.dot(pre_grad, inner_rows, preferred_element_type=jnp.float32)
    unit_grads = jnp.stack(
        [inner_rows_grad.astype(jnp.bfloat16), outer_proj_grad.astype(jnp.bfloat16)]
    )
    unit_grads = lax.psum_scatter(unit_grads, "ffn", scatter_dimension=1, tiled=True)
    unit_grads = lax.psum(unit_grads, "tok").astype(jnp.float32)
    inner_proj_grad, outer_proj_grad = (unit_grads[0].T, unit_grads[1])
    first_grad = sum_grad + first_back
    attn_sum_grad, first_gain_grad, first_shift_grad = normalize_back(
        first_grad, first_normed, first_scale, first_gain
    )
    attn_grad = attn_sum_grad.astype(jnp.bfloat16)
    out_bias_grad = jnp.sum(attn_grad.astype(jnp.float32), axis=0)
    out_proj_grad = contract_rows(context_low, attn_grad)
    context_grad = (
        contract_cols(attn_grad, out_proj)
        .astype(jnp.bfloat16)
        .reshape(seq_rows, seq_len, HEADS, DH)
    )
    context_grad = context_grad * head_on.astype(jnp.bfloat16)[:, None]
    scores = scores_of(queries, key_heads)
    probs = jnp.exp(scores - log_total)
    probs_again = probs.astype(jnp.bfloat16)
    value_part = jnp.einsum(
        "rhqk,rqhd->rkhd", probs_again, context_grad, preferred_element_type=jnp.float32
    )
    prob_grad = jnp.einsum(
        "rqhd,rkhd->rhqk", context_grad, value_heads, preferred_element_type=jnp.float32
    )
    score_grad = (probs * (prob_grad - jnp.sum(probs * prob_grad, axis=-1, keepdims=True))).astype(
        jnp.bfloat16
    )
    query_part = (
        jnp.einsum("rhqk,rkhd->rqhd", score_grad, key_heads, preferred_element_type=jnp.float32)
        * factor
    )
    key_part = (
        jnp.einsum("rhqk,rqhd->rkhd", score_grad, queries, preferred_element_type=jnp.float32)
        * factor
    )
    joint_grad = (
        jnp.stack([query_part, key_part, value_part], axis=2)
        .astype(jnp.bfloat16)
        .reshape(tok_rows, 3 * model_width)
    )
    joint_bias_grad = jnp.sum(joint_grad.astype(jnp.float32), axis=0)
    query_bias_grad = joint_bias_grad[:model_width]
    value_bias_grad = joint_bias_grad[2 * model_width :]
    joint_proj_grad = contract_rows(tokens, joint_grad)
    input_grad = attn_sum_grad + contract_cols(joint_grad, joint_proj)
    joint_proj_grad, out_proj_grad = lax.psum(
        (joint_proj_grad.astype(jnp.bfloat16), out_proj_grad.astype(jnp.bfloat16)), ("ffn", "tok")
    )
    joint_proj_grad = joint_proj_grad.astype(jnp.float32)
    out_proj_grad = out_proj_grad.astype(jnp.float32)
    small = [
        query_bias_grad,
        value_bias_grad,
        out_bias_grad,
        first_gain_grad,
        first_shift_grad,
        outer_bias_grad,
        second_gain_grad,
        second_shift_grad,
        inner_bias_sum,
    ]
    small = lax.psum(jnp.concatenate(small), ("ffn", "tok"))
    (
        query_bias_grad,
        value_bias_grad,
        out_bias_grad,
        first_gain_grad,
        first_shift_grad,
        outer_bias_grad,
        second_gain_grad,
        second_shift_grad,
    ) = [small[i * model_width : (i + 1) * model_width] for i in range(8)]
    inner_bias_grad = lax.dynamic_slice(
        small, (8 * model_width + ffn_place * unit_share,), (unit_share,)
    )
    return (
        output,
        cls_states,
        input_grad,
        joint_proj_grad,
        query_bias_grad,
        value_bias_grad,
        out_proj_grad,
        out_bias_grad,
        first_gain_grad,
        first_shift_grad,
        inner_proj_grad,
        inner_bias_grad,
        outer_proj_grad,
        outer_bias_grad,
        second_gain_grad,
        second_shift_grad,
    )


def solution(mesh):
    return jax.shard_map(
        on_device,
        mesh=mesh,
        in_specs=(
            P(("ffn", "tok"), None),
            P(),
            P(),
            P(),
            P(),
            P(),
            P(),
            P(),
            P(None, "ffn"),
            P("ffn"),
            P("ffn", None),
            P(),
            P(),
            P(),
            P(("ffn", "tok")),
            P(("ffn", "tok"), None),
            P(),
            P(("ffn", "tok"), None),
        ),
        out_specs=(
            P(("ffn", "tok"), None),
            P(("ffn", "tok"), None, None),
            P(("ffn", "tok"), None),
            P(),
            P(),
            P(),
            P(),
            P(),
            P(),
            P(),
            P(None, "ffn"),
            P("ffn"),
            P("ffn", None),
            P(),
            P(),
            P(),
        ),
        check_vma=False,
    )
```

profile of v0, /device:TPU:0, one launch (start us, length us, event | category | flops | bytes accessed | tf_op | source)
XLA Modules:
  0.0 448.7 jit_solution(7823230462201781648)
XLA Ops:
  7.2 2.1 pad_maximum_fusion.1
  9.4 1.3 convert_element_type.152
  10.7 1.3 convert_element_type.157
  14.7 37.2 %all-reduce = bf16[3072]{0:T(1024)(128)(2,1)S(1)} all-reduce(bf16[3072]{0:T(1024)(128)(2,1)S(1)} %dynamic-update-slice), channel_id=1, replica_groups=mesh['ffn'=16,'tok'=2] {'ffn'}, use_global_device_ids=true, to_apply=%add | all-reduce | flops 3072 | bytes 12288
  53.2 4.5 %fusion.22 = bf16[512,2304]{1,0:T(8,128)(2,1)} fusion(bf16[512,768]{1,0:T(8,128)(2,1)} %param.18, bf16[768,2304]{1,0:T(8,128)(2,1)S(1)} %copy-done, f32[2304]{0:T(1024)S(1)} %maximum_convert_fusion.1), kind=kOutput, calls=%fused_computation.48 | convolution fusion | flops 1814298624 | bytes 6693888 | tf_op jit(solution)/shard_map/dot_general | solution.py:89
  57.7 4.3 copy.43
  64.7 1.2 fusion.45
  66.2 3.5 fusion
  69.7 3.7 exponential_reduce_fusion
  74.3 4.8 %fusion.34 = bf16[1,12,64,512]{3,2,1,0:T(8,128)(2,1)S(1)} fusion(f32[12]{0:T(128)S(1)} %get-tuple-element.95, bf16[1,512,3,12,64]{1,4,3,2,0:T(8,128)(2,1)} %bitcast.110, f32[12,512,512]{1,2,0:T(8,128)S(1)} %get-tuple-element.83, f32[12,512]{1,0:T(8,128)S(1)} %log_add_fusion, pred[512,512]{0,1:T(8,128)(4,1)} %copy-done.3), kind=kOutput, calls=%fused_computation.64 | convolution fusion | flops 416022528 | bytes 14442544 | tf_op jit(solution)/shard_map/rhqk,rkhd->rqhd/dot_general | solution.py:110
  82.1 13.0 %all-gather.2.cloned.1.call-done = bf16[2,3072,768]{2,1,0:T(8,128)(2,1)} async-done(((bf16[2,192,768]{2,1,0:T(8,128)(2,1)}), bf16[2,3072,768]{2,1,0:T(8,128)(2,1)}) %all-gather.2.cloned.1.call-update) | async-done | bytes 9437200 | tf_op jit(solution)/shard_map/all_gather | solution.py:120
  95.1 18.9 %fusion.5 = (bf16[512,3072]{1,0:T(8,128)(2,1)S(1)}, f32[512,3072]{1,0:T(8,128)S(1)}) fusion(f32[3072]{0:T(1024)} %fusion.45, f32[3072]{0:T(1024)S(1)} %copy-done.19, bf16[2,3072,768]{2,1,0:T(8,128)(2,1)} %all-gather.2.cloned.1.call-done, f32[512,768]{1,0:T(8,128)} %copy-done.7, f32[768]{0:T(1024)} %param.25, f32[768]{0:T(1024)} %param.24, ...), kind=kOutput, calls=%fused_computation.14 | convolution fusion | flops 2523267072 | bytes 15765504 | tf_op jit(solution)/shard_map/dot_general | solution.py:46
  114.1 2.8 fusion.65
  117.2 1.3 fusion.33
  118.5 2.7 convert_reduce_fusion.3
  121.2 4.4 fusion.21
  125.5 6.3 %convert_reduce_fusion = (f32[3072]{0:T(1024)}, bf16[512,3072]{1,0:T(8,128)(2,1)S(1)}) fusion(f32[3072]{0:T(1024)S(1)} %copy-done.20, f32[512,3072]{1,0:T(8,128)S(1)} %get-tuple-element.87, f32[3072]{0:T(1024)S(1)} %copy-done.19, bf16[2,3072,768]{2,1,0:T(8,128)(2,1)S(1)} %copy-done.31, f32[512,768]{1,0:T(8,128)S(1)} %get-tuple-element.61), kind=kOutput, calls=%fused_computation.22 | convolution fusion | flops 2438329344 | bytes 15765504 | tf_op jit(solution)/shard_map/dot_general | solution.py:46
  131.9 1.7 copy-done.38
  133.5 5.0 %fusion.20 = bf16[1,3072,768]{2,1,0:T(8,128)(2,1)} fusion(bf16[512,3072]{1,0:T(8,128)(2,1)S(1)} %get-tuple-element.94, f32[512,768]{1,0:T(8,128)S(1)} %copy-done.8, f32[768]{0:T(1024)S(1)} %copy-done.36, f32[768]{0:T(1024)S(1)} %copy-done.24, f32[512]{0:T(512)S(1)} %copy-done.22, f32[512]{0:T(512)S(1)} %broadcast_multiply_fusion.5), kind=kOutput, calls=%fused_computation.46 | convolution fusion | flops 2420244480 | bytes 9447424 | tf_op jit(solution)/shard_map/dot_general | solution.py:40
  138.6 8.2 %pad_maximum_fusion = bf16[2,3072,768]{2,1,0:T(8,128)(2,1)} fusion(bf16[1,3072,768]{2,1,0:T(8,128)(2,1)} %fusion.21, bf16[1,3072,768]{2,1,0:T(8,128)(2,1)} %fusion.20), kind=kLoop, calls=%fused_computation.9 | loop fusion | flops 4718592 | bytes 18874368 | tf_op jit(solution)/shard_map/stack | solution.py:146
  147.5 8.3 %multiply_reduce_fusion.1 = (f32[768]{0:T(1024)}, f32[512]{0:T(512)S(1)}, f32[512]{0:T(512)S(1)}, f32[768]{0:T(1024)}, f32[512,768]{1,0:T(8,128)S(1)}) fusion(f32[512,768]{1,0:T(8,128)} %copy-done.7, f32[512]{0:T(512)S(1)} %copy-done.23, f32[512]{0:T(512)S(1)} %broadcast_multiply_fusion.5, f32[768]{0:T(1024)S(1)} %copy-done.25, f32[512,768]{1,0:T(8,128)} %copy-done.13, ...), kind=kOutput, calls=%fused_computation.66 | convolution fusion | flops 2419848704 | bytes 12600320 | tf_op jit(solution)/shard_map/dot_general | solution.py:145
  158.0 1.7 convolution_convert_fusion.4
  159.7 2.4 copy.45
  162.2 14.8 %multiply_reduce_fusion = (f32[12,512]{1,0:T(8,128)S(1)}, f32[12,512,512]{1,2,0:T(8,128)}) fusion(f32[12,512,512]{1,2,0:T(8,128)} %copy-done.1, f32[12,512]{1,0:T(8,128)} %copy-done.16, pred[512,512]{0,1:T(8,128)(4,1)} %copy-done.3, bf16[1,512,3,12,64]{1,4,3,2,0:T(8,128)(2,1)} %bitcast.111, bf16[512,12,64]{0,2,1:T(8,128)(2,1)} %bitcast.114, ...), kind=kOutput, calls=%fused_computation.2 | convolution fusion | flops 418768896 | bytes 27058200 | tf_op jit(solution)/shard_map/rqhd,rkhd->rhqk/dot_general | solution.py:171
  177.1 7.7 %multiply_convert_fusion = bf16[12,512,512]{1,2,0:T(8,128)(2,1)S(1)} fusion(f32[12,512,512]{1,2,0:T(8,128)} %get-tuple-element.92, f32[12,512,512]{1,2,0:T(8,128)S(1)} %bitcast.108, f32[12,512]{1,0:T(8,128)S(1)} %get-tuple-element.91, f32[12,512]{1,0:T(8,128)S(1)} %copy-done.17, pred[512,512]{0,1:T(8,128)(4,1)S(1)} %copy-done.4), kind=kLoop, calls=%fused_computation.1 | loop fusion | flops 18874368 | bytes 31768576 | tf_op jit(solution)/shard_map/convert_element_type | solution.py:174
  184.8 2.0 multiply_bitcast_fusion
  188.0 3.7 convolution_bitcast_fusion
  193.3 1.8 convolution_convert_fusion.3
  195.1 3.8 fusion.23
  202.1 2.1 gather_fusion
  204.2 1.3 constant_dynamic-update-slice_fusion.8
  205.5 1.3 constant_dynamic-update-slice_fusion.7
  206.8 1.3 constant_dynamic-update-slice_fusion.6
  208.1 1.3 constant_dynamic-update-slice_fusion.5
  209.5 1.3 constant_dynamic-update-slice_fusion.4
  210.8 1.3 constant_dynamic-update-slice_fusion.3
  212.1 1.3 constant_dynamic-update-slice_fusion.2
  213.4 1.3 constant_dynamic-update-slice_fusion.1
  214.7 1.3 constant_dynamic-update-slice_fusion
  216.0 41.3 %psum.29 = f32[9216]{0:T(1024)} all-reduce(f32[9216]{0:T(1024)} %constant_dynamic-update-slice_fusion), channel_id=1, replica_groups=mesh['ffn'=16,'tok'=2] {'ffn','tok'}, use_global_device_ids=true, to_apply=%region_22.23 | all-reduce | flops 9216 | bytes 73728 | tf_op jit(solution)/shard_map/psum | solution.py:211
  257.3 1.3 dynamic_slice.3
  258.6 1.3 bitcast_select_fusion
  259.9 1.4 fusion.62
  261.4 5.3 %convolution_add_fusion.1 = f32[512,768]{1,0:T(8,128)} fusion(f32[512,768]{1,0:T(8,128)} %copy-done.5, bf16[512,2304]{0,1:T(8,128)(2,1)} %bitcast.117, bf16[768,2304]{1,0:T(8,128)(2,1)S(1)} %copy-done), kind=kOutput, calls=%fused_computation.83 | convolution fusion | flops 1812332544 | bytes 9043968 | tf_op jit(solution)/shard_map/dot_general | solution.py:46
  266.7 142.0 %all-reduce.7.cloned.1.call-done = (bf16[768,2304]{0,1:T(8,128)(2,1)}, bf16[768,768]{1,0:T(8,128)(2,1)}) async-done(((bf16[768,2304]{0,1:T(8,128)(2,1)}, bf16[768,768]{1,0:T(8,128)(2,1)}), (bf16[768,2304]{0,1:T(8,128)(2,1)}, bf16[768,768]{1,0:T(8,128)(2,1)})) %all-reduce.7.cloned.1.call-update) | async-done | bytes 4718608 | tf_op jit(solution)/shard_map/psum | solution.py:195
  408.7 2.8 convert_element_type.176
  411.5 5.9 %copy.49 = f32[768,2304]{1,0:T(8,128)} copy(bf16[768,2304]{0,1:T(8,128)(2,1)} %get-tuple-element.58) | data formatting | bytes 10616832
  417.5 22.3 %all-reduce.5.cloned.1.call-done = bf16[2,192,768]{2,1,0:T(8,128)(2,1)} async-done(((bf16[2,192,768]{2,1,0:T(8,128)(2,1)}), bf16[2,192,768]{2,1,0:T(8,128)(2,1)}) %all-reduce.5.cloned.1.call-update) | async-done | bytes 589840 | tf_op jit(solution)/shard_map/psum | solution.py:150
  (128 shorter events, 21.7 us)
Async XLA Ops:
  7.2 46.0 %copy-start = (bf16[768,2304]{1,0:T(8,128)(2,1)S(1)}, bf16[768,2304]{1,0:T(8,128)(2,1)}, u32[]{:S(2)}) copy-start(bf16[768,2304]{1,0:T(8,128)(2,1)} %param.19) | copy-start | bytes 10616836
  7.2 87.9 %all-gather.2.cloned.1.call-start = ((), (), s32[]{:S(2)}) async-start(), calls=%async_computation.1 | async-start | bytes 10027008 | tf_op jit(solution)/shard_map/all_gather | solution.py:120
  9.3 252.0 %reduce-scatter.2.cloned.1.call-start = ((), (), s32[]{:S(2)}) async-start(), calls=%async_computation.2 | async-start | bytes 10027008 | tf_op jit(solution)/shard_map/reduce_scatter | solution.py:149
  57.7 4.3 copy-start.28
  57.7 8.2 %copy-start.21 = (s32[512]{0:T(512)S(1)}, s32[512]{0:T(512)}, u32[]{:S(2)}) copy-start(s32[512]{0:T(512)} %param.32) | copy-start | bytes 6148
  66.1 3.5 copy-start.3
  69.7 4.6 %copy-start.1 = (f32[12,512,512]{1,2,0:T(8,128)}, f32[12,512,512]{1,2,0:T(8,128)S(1)}, u32[]{:S(2)}) copy-start(f32[12,512,512]{1,2,0:T(8,128)S(1)} %get-tuple-element.83) | copy-start | bytes 37748740
  73.4 5.6 %copy-start.16 = (f32[12,512]{1,0:T(8,128)}, f32[12,512]{1,0:T(8,128)S(1)}, u32[]{:S(2)}) copy-start(f32[12,512]{1,0:T(8,128)S(1)} %log_add_fusion) | copy-start | bytes 73732
  74.3 4.8 %copy-start.27 = (f32[768]{0:T(1024)S(1)}, f32[768]{0:T(1024)}, u32[]{:S(2)}) copy-start(f32[768]{0:T(1024)} %convert_element_type.152) | copy-start | bytes 9220
  74.3 4.8 %copy-start.32 = (bf16[768,768]{1,0:T(8,128)(2,1)S(1)}, bf16[768,768]{1,0:T(8,128)(2,1)}, u32[]{:S(2)}) copy-start(bf16[768,768]{1,0:T(8,128)(2,1)} %param.22) | copy-start | bytes 3538948
  74.3 4.8 %copy-start.34 = (bf16[512,768]{1,0:T(8,128)(2,1)S(1)}, bf16[512,768]{1,0:T(8,128)(2,1)}, u32[]{:S(2)}) copy-start(bf16[512,768]{1,0:T(8,128)(2,1)} %param.18) | copy-start | bytes 2359300
  79.1 2.4 copy-start.14
  79.1 16.0 %copy-start.19 = (f32[3072]{0:T(1024)S(1)}, f32[3072]{0:T(1024)}, u32[]{:S(2)}) copy-start(f32[3072]{0:T(1024)} %convert_element_type.154) | copy-start | bytes 36868
  80.0 1.1 copy-start.7
  95.1 18.9 %copy-start.8 = (f32[512,768]{1,0:T(8,128)S(1)}, f32[512,768]{1,0:T(8,128)}, u32[]{:S(2)}) copy-start(f32[512,768]{1,0:T(8,128)} %copy-done.7) | copy-start | bytes 4718596
  95.1 18.9 %copy-start.22 = (f32[512]{0:T(512)S(1)}, f32[512]{0:T(512)}, u32[]{:S(2)}) copy-start(f32[512]{0:T(512)} %add_rsqrt_fusion.1) | copy-start | bytes 6148
  95.1 18.9 %copy-start.24 = (f32[768]{0:T(1024)S(1)}, f32[768]{0:T(1024)}, u32[]{:S(2)}) copy-start(f32[768]{0:T(1024)} %param.24) | copy-start | bytes 9220
  95.1 18.9 %copy-start.26 = (f32[768]{0:T(1024)S(1)}, f32[768]{0:T(1024)}, u32[]{:S(2)}) copy-start(f32[768]{0:T(1024)} %convert_element_type.157) | copy-start | bytes 9220
  95.1 18.9 %copy-start.31 = (bf16[2,3072,768]{2,1,0:T(8,128)(2,1)S(1)}, bf16[2,3072,768]{2,1,0:T(8,128)(2,1)}, u32[]{:S(2)}) copy-start(bf16[2,3072,768]{2,1,0:T(8,128)(2,1)} %all-gather.2.cloned.1.call-done) | copy-start | bytes 28311556
  95.1 18.9 %copy-start.36 = (f32[768]{0:T(1024)S(1)}, f32[768]{0:T(1024)}, u32[]{:S(2)}) copy-start(f32[768]{0:T(1024)} %param.25) | copy-start | bytes 9220
  114.1 3.1 copy-start.11
  114.1 3.1 copy-start.18
  114.1 4.4 copy-start.29
  121.2 4.4 copy-start.13
  121.2 4.4 copy-start.20
  131.9 1.7 copy-start.38
  146.8 0.7 copy-start.23
  146.8 0.7 copy-start.25
  146.8 261.9 %all-reduce.7.cloned.1.call-start = ((), (), s32[]{:S(2)}) async-start(), calls=%async_computation.4 | async-start | bytes 9437184 | tf_op jit(solution)/shard_map/psum | solution.py:195
  147.5 8.3 %copy-start.9 = (f32[512,768]{1,0:T(8,128)S(1)}, f32[512,768]{1,0:T(8,128)}, u32[]{:S(2)}) copy-start(f32[512,768]{1,0:T(8,128)} %copy-done.7) | copy-start | bytes 4718596
  155.8 2.3 copy-start.33
  155.8 6.4 %copy-start.30 = (bf16[12]{0:T(256)(128)(2,1)S(1)}, bf16[12]{0:T(256)(128)(2,1)}, u32[]{:S(2)}) copy-start(bf16[12]{0:T(256)(128)(2,1)} %get-tuple-element.96) | copy-start | bytes 76
  156.9 1.1 copy-start.5
  162.1 14.9 %slice-start = ((s8[12582912]{0:T(1024)(128)(4,1)}), s8[4194304]{0:T(1024)(128)(4,1)S(1)}, s32[]{:S(2)}) async-start(s8[12582912]{0:T(1024)(128)(4,1)} %bitcast.107), calls=%async_computation.5 | async-start | bytes 8388608
  162.1 14.9 %slice-start.1 = ((s8[12582912]{0:T(1024)(128)(4,1)}), s8[4194304]{0:T(1024)(128)(4,1)S(1)}, s32[]{:S(2)}) async-start(s8[12582912]{0:T(1024)(128)(4,1)} %bitcast.107), calls=%async_computation.6 | async-start | bytes 8388608
  162.1 14.9 %slice-start.2 = ((s8[12582912]{0:T(1024)(128)(4,1)}), s8[4194304]{0:T(1024)(128)(4,1)S(1)}, s32[]{:S(2)}) async-start(s8[12582912]{0:T(1024)(128)(4,1)} %bitcast.107), calls=%async_computation.7 | async-start | bytes 8388608
  162.1 14.9 %copy-start.4 = (pred[512,512]{0,1:T(8,128)(4,1)S(1)}, pred[512,512]{0,1:T(8,128)(4,1)}, u32[]{:S(2)}) copy-start(pred[512,512]{0,1:T(8,128)(4,1)} %copy-done.3) | copy-start | bytes 786436
  162.2 14.9 %copy-start.17 = (f32[12,512]{1,0:T(8,128)S(1)}, f32[12,512]{1,0:T(8,128)}, u32[]{:S(2)}) copy-start(f32[12,512]{1,0:T(8,128)} %copy-done.16) | copy-start | bytes 73732
  177.0 7.8 %copy-start.2 = (bf16[512,2304]{0,1:T(8,128)(2,1)S(1)}, bf16[512,2304]{0,1:T(8,128)(2,1)}, u32[]{:S(2)}) copy-start(bf16[512,2304]{0,1:T(8,128)(2,1)} %copy.43) | copy-start | bytes 7077892
  186.8 1.1 copy-start.10
  191.7 1.4 copy-start.6
  191.7 1.6 copy-start.15
  191.7 3.4 copy-start.35
  193.3 1.8 copy-start.12
  198.9 0.7 copy-start.37
  198.9 240.8 %all-reduce.5.cloned.1.call-start = ((), (), s32[]{:S(2)}) async-start(), calls=%async_computation.3 | async-start | bytes 1179648 | tf_op jit(solution)/shard_map/psum | solution.py:150
Sparse Core Ops, SparseCore 0:
  10.9 84.1 all-gather.1
  146.9 110.6 reduce-scatter.1
  264.0 144.5 all-reduce.6
  410.8 28.8 all-reduce.4
where the time goes:
time: 457 us; the launch traced here: 449 us
  waiting for transfers between devices  177 us (39%)
  matrix products  93.7 us (21%)
  blocking collectives  78.5 us (17%)
  other arithmetic  43.2 us (9%)
  local copies, waits for them, and re-layouts  40.8 us (9%)
  between operations  15.1 us (3%)
    psum x1, waiting for transfers between devices, on_device(): lax.psum((joint_proj_grad.astype(jnp.bfloat16), out_proj_grad.astype(jnp....  142 us
    psum x1, blocking collectives, on_device(): small = lax.psum(jnp.concatenate(small), ('ffn', 'tok'))  41.3 us
    unnamed x1, blocking collectives  37.2 us
    dot_general x4, matrix products, contract_cols(): lax.dot_general(left_side, right_side, (((1,), (1,)), ((), ())), preferre...  32.2 us
    unnamed x96, local copies, waits for them, and re-layouts  25.2 us
    psum x1, waiting for transfers between devices, on_device(): unit_grads = lax.psum(unit_grads, 'tok').astype(jnp.float32)  22.3 us
    dot_general x4, matrix products, contract_rows(): lax.dot_general(left_side, right_side, (((0,), (0,)), ((), ())), preferre...  15 us
    dot_general x1, matrix products, on_device(): jnp.einsum('rqhd,rkhd->rhqk', context_grad, value_heads, preferred_elemen...  14.8 us
  transfers between devices with their start and end apart: 4, of which 3 were waited for; matrix products, arithmetic and copies ran while one was open for 26% of the time, Pallas kernels for 0%

commit v1 on v0

--- a/solution.py
+++ b/solution.py
@@ -208,7 +208,7 @@
         second_shift_grad,
         inner_bias_sum,
     ]
-    small = lax.psum(jnp.concatenate(small), ("ffn", "tok"))
+    small = jnp.sum(lax.all_gather(jnp.concatenate(small), ("ffn", "tok")), axis=0)
     (
         query_bias_grad,
         value_bias_grad,

time: 457 us -> 512 us (1.12)
  waiting for transfers between devices: 177 us -> 267 us
  blocking collectives: 78.5 us -> 37.2 us
    all_gather x0 -> x1, waiting for transfers between devices: none -> 48.6 us  [on_device(): lax.all_gather(jnp.concatenate(small), ('ffn', 'tok'))]
    psum x1 -> x0, blocking collectives: 41.3 us -> none  [on_device(): small = lax.psum(jnp.concatenate(small), ('ffn', 'tok'))]
    reduce_scatter x1, waiting for transfers between devices: 0.01 us -> 40.1 us  [on_device(): lax.psum_scatter(unit_grads, 'ffn', scatter_dimension=1, tiled=True)]
    unnamed x96 -> x88, local copies, waits for them, and re-layouts: 25.2 us -> 24.6 us
  transfers between devices with their start and end apart: 4 -> 5, of which waited for: 3 -> 5; matrix products, arithmetic and copies ran while one was open for 26% -> 25% of each run, Pallas kernels for 0% -> 0%
where the time goes in v1:
time: 512 us; the launch traced here: 504 us
  waiting for transfers between devices  267 us (52%)
  matrix products  97.3 us (19%)
  other arithmetic  45.3 us (9%)
  local copies, waits for them, and re-layouts  41.8 us (8%)
  blocking collectives  37.2 us (7%)
  between operations  15.1 us (3%)
    psum x1, waiting for transfers between devices, on_device(): lax.psum((joint_proj_grad.astype(jnp.bfloat16), out_proj_grad.astype(jnp....  143 us
    all_gather x1, waiting for transfers between devices, on_device(): lax.all_gather(jnp.concatenate(small), ('ffn', 'tok'))  48.6 us
    reduce_scatter x1, waiting for transfers between devices, on_device(): lax.psum_scatter(unit_grads, 'ffn', scatter_dimension=1, tiled=True)  40.1 us
    unnamed x1, blocking collectives  37.2 us
    dot_general x4, matrix products, contract_cols(): lax.dot_general(left_side, right_side, (((1,), (1,)), ((), ())), preferre...  32.2 us
    unnamed x88, local copies, waits for them, and re-layouts  24.6 us
    psum x1, waiting for transfers between devices, on_device(): unit_grads = lax.psum(unit_grads, 'tok').astype(jnp.float32)  22.2 us
    dot_general x4, matrix products, contract_rows(): lax.dot_general(left_side, right_side, (((0,), (0,)), ((), ())), preferre...  18.6 us
  transfers between devices with their start and end apart: 5, of which 5 were waited for; matrix products, arithmetic and copies ran while one was open for 25% of the time, Pallas kernels for 0%

profile of v1, /device:TPU:0, one launch (start us, length us, event | category | flops | bytes accessed | tf_op | source)
XLA Modules:
  0.0 504.0 jit_solution(7329370030291426157)
XLA Ops:
  7.2 2.1 pad_maximum_fusion.1
  14.7 37.2 %all-reduce = bf16[3072]{0:T(1024)(128)(2,1)S(1)} all-reduce(bf16[3072]{0:T(1024)(128)(2,1)S(1)} %dynamic-update-slice), channel_id=1, replica_groups=mesh['ffn'=16,'tok'=2] {'ffn'}, use_global_device_ids=true, to_apply=%add | all-reduce | flops 3072 | bytes 12288
  53.2 4.5 fusion.22
  57.7 4.3 copy.57
  66.2 3.5 fusion
  69.7 3.7 exponential_reduce_fusion
  74.3 4.8 fusion.34
  82.1 13.0 %all-gather.4.cloned.1.call-done = bf16[2,3072,768]{2,1,0:T(8,128)(2,1)} async-done(((bf16[2,192,768]{2,1,0:T(8,128)(2,1)}), bf16[2,3072,768]{2,1,0:T(8,128)(2,1)}) %all-gather.4.cloned.1.call-update) | async-done | bytes 9437200 | tf_op jit(solution)/shard_map/all_gather | solution.py:120
  95.1 18.9 %fusion.5 = (bf16[512,3072]{1,0:T(8,128)(2,1)S(1)}, f32[512,3072]{1,0:T(8,128)S(1)}) fusion(f32[3072]{0:T(1024)} %fusion.45, f32[3072]{0:T(1024)S(1)} %copy-done.16, bf16[2,3072,768]{2,1,0:T(8,128)(2,1)} %all-gather.4.cloned.1.call-done, f32[512,768]{1,0:T(8,128)} %copy-done.6, f32[768]{0:T(1024)} %param.25, f32[768]{0:T(1024)} %param.24, ...), kind=kOutput, calls=%fused_computation.14 | convolution fusion | flops 2523267072 | bytes 15765504 | tf_op jit(solution)/shard_map/dot_general | solution.py:46
  114.1 2.8 fusion.65
  118.5 2.7 convert_reduce_fusion.3
  121.2 4.4 fusion.21
  125.5 6.3 %convert_reduce_fusion = (f32[3072]{0:T(1024)}, bf16[512,3072]{1,0:T(8,128)(2,1)S(1)}) fusion(f32[3072]{0:T(1024)S(1)} %copy-done.17, f32[512,3072]{1,0:T(8,128)S(1)} %get-tuple-element.119, f32[3072]{0:T(1024)S(1)} %copy-done.16, bf16[2,3072,768]{2,1,0:T(8,128)(2,1)S(1)} %copy-done.28, f32[512,768]{1,0:T(8,128)S(1)} %get-tuple-element.93), kind=kOutput, calls=%fused_computation.22 | convolution fusion | flops 2438329344 | bytes 15765504 | tf_op jit(solution)/shard_map/dot_general | solution.py:46
  131.9 1.7 copy-done.34
  133.5 5.0 fusion.20
  138.6 8.2 %pad_maximum_fusion = bf16[2,3072,768]{2,1,0:T(8,128)(2,1)} fusion(bf16[1,3072,768]{2,1,0:T(8,128)(2,1)} %fusion.21, bf16[1,3072,768]{2,1,0:T(8,128)(2,1)} %fusion.20), kind=kLoop, calls=%fused_computation.9 | loop fusion | flops 4718592 | bytes 18874368 | tf_op jit(solution)/shard_map/stack | solution.py:146
  147.5 8.3 %multiply_reduce_fusion.1 = (f32[768]{0:T(1024)}, f32[512]{0:T(512)S(1)}, f32[512]{0:T(512)S(1)}, f32[768]{0:T(1024)}, f32[512,768]{1,0:T(8,128)S(1)}) fusion(f32[512,768]{1,0:T(8,128)} %copy-done.6, f32[512]{0:T(512)S(1)} %copy-done.20, f32[512]{0:T(512)S(1)} %broadcast_multiply_fusion.5, f32[768]{0:T(1024)S(1)} %copy-done.22, f32[512,768]{1,0:T(8,128)} %copy-done.11, ...), kind=kOutput, calls=%fused_computation.66 | convolution fusion | flops 2419848704 | bytes 12600320 | tf_op jit(solution)/shard_map/dot_general | solution.py:145
  158.0 1.7 convolution_convert_fusion.4
  159.7 2.4 copy.59
  162.2 14.8 %multiply_reduce_fusion = (f32[12,512]{1,0:T(8,128)S(1)}, f32[12,512,512]{1,2,0:T(8,128)}) fusion(f32[12,512,512]{1,2,0:T(8,128)} %copy-done.1, f32[12,512]{1,0:T(8,128)} %copy-done.13, pred[512,512]{0,1:T(8,128)(4,1)} %copy-done.3, bf16[1,512,3,12,64]{1,4,3,2,0:T(8,128)(2,1)} %bitcast.111, bf16[512,12,64]{0,2,1:T(8,128)(2,1)} %bitcast.114, ...), kind=kOutput, calls=%fused_computation.2 | convolution fusion | flops 418768896 | bytes 27058200 | tf_op jit(solution)/shard_map/rqhd,rkhd->rhqk/dot_general | solution.py:171
  177.1 7.7 %multiply_convert_fusion = bf16[12,512,512]{1,2,0:T(8,128)(2,1)S(1)} fusion(f32[12,512,512]{1,2,0:T(8,128)} %get-tuple-element.124, f32[12,512,512]{1,2,0:T(8,128)S(1)} %bitcast.108, f32[12,512]{1,0:T(8,128)S(1)} %get-tuple-element.123, f32[12,512]{1,0:T(8,128)S(1)} %copy-done.14, pred[512,512]{0,1:T(8,128)(4,1)S(1)} %copy-done.4), kind=kLoop, calls=%fused_computation.1 | loop fusion | flops 18874368 | bytes 31768576 | tf_op jit(solution)/shard_map/convert_element_type | solution.py:174
  184.8 2.0 multiply_bitcast_fusion
  188.0 3.7 convolution_bitcast_fusion
  191.7 1.7 convert_reduce_fusion.1
  194.1 1.3 constant_dynamic-update-slice_fusion.8
  195.4 1.3 constant_dynamic-update-slice_fusion.7
  196.7 1.3 constant_dynamic-update-slice_fusion.6
  198.1 1.3 constant_dynamic-update-slice_fusion.5
  199.4 1.3 constant_dynamic-update-slice_fusion.4
  200.7 1.3 constant_dynamic-update-slice_fusion.3
  202.0 1.3 constant_dynamic-update-slice_fusion.2
  203.3 1.3 constant_dynamic-update-slice_fusion.1
  204.6 1.3 constant_dynamic-update-slice_fusion
  206.0 3.5 convolution_convert_fusion.3
  209.4 5.7 %fusion.23 = bf16[768,2304]{0,1:T(8,128)(2,1)} fusion(bf16[512,2304]{0,1:T(8,128)(2,1)} %bitcast.116, bf16[512,768]{1,0:T(8,128)(2,1)} %param.18), kind=kOutput, calls=%fused_computation.49 | convolution fusion | flops 1813708800 | bytes 6684672 | tf_op jit(solution)/shard_map/dot_general | solution.py:40
  216.4 40.1 %reduce-scatter.2.cloned.1.call-done = bf16[2,192,768]{2,1,0:T(8,128)(2,1)} async-done(((bf16[2,3072,768]{2,1,0:T(8,128)(2,1)}), bf16[2,192,768]{2,1,0:T(8,128)(2,1)}) %reduce-scatter.2.cloned.1.call-update) | async-done | bytes 589840 | tf_op jit(solution)/shard_map/reduce_scatter | solution.py:149
  256.5 5.3 %convolution_add_fusion.1 = f32[512,768]{1,0:T(8,128)} fusion(f32[512,768]{1,0:T(8,128)} %copy-done.5, bf16[512,2304]{0,1:T(8,128)(2,1)} %bitcast.117, bf16[768,2304]{1,0:T(8,128)(2,1)S(1)} %copy-done), kind=kOutput, calls=%fused_computation.83 | convolution fusion | flops 1812332544 | bytes 9043968 | tf_op jit(solution)/shard_map/dot_general | solution.py:46
  261.8 2.0 gather_fusion
  263.8 1.3 bitcast_select_fusion
  265.1 48.6 %all-gather.6.cloned.1.call-done = f32[294912]{0:T(1024)} async-done(((f32[9216]{0:T(1024)}), f32[294912]{0:T(1024)}) %all-gather.6.cloned.1.call-update) | async-done | bytes 1179664 | tf_op jit(solution)/shard_map/all_gather | solution.py:211
  313.7 2.5 reshape.412
  316.2 2.0 reduce_sum.209
  318.2 1.3 dynamic_slice.3
  319.5 1.4 fusion.62
  320.9 143.0 %all-reduce.7.cloned.1.call-done = (bf16[768,2304]{0,1:T(8,128)(2,1)}, bf16[768,768]{1,0:T(8,128)(2,1)}) async-done(((bf16[768,2304]{0,1:T(8,128)(2,1)}, bf16[768,768]{1,0:T(8,128)(2,1)}), (bf16[768,2304]{0,1:T(8,128)(2,1)}, bf16[768,768]{1,0:T(8,128)(2,1)})) %all-reduce.7.cloned.1.call-update) | async-done | bytes 4718608 | tf_op jit(solution)/shard_map/psum | solution.py:195
  464.0 2.8 convert_element_type.176
  466.8 5.9 %copy.63 = f32[768,2304]{1,0:T(8,128)} copy(bf16[768,2304]{0,1:T(8,128)(2,1)} %get-tuple-element.90) | data formatting | bytes 10616832
  472.8 22.2 %all-reduce.5.cloned.1.call-done = bf16[2,192,768]{2,1,0:T(8,128)(2,1)} async-done(((bf16[2,192,768]{2,1,0:T(8,128)(2,1)}), bf16[2,192,768]{2,1,0:T(8,128)(2,1)}) %all-reduce.5.cloned.1.call-update) | async-done | bytes 589840 | tf_op jit(solution)/shard_map/psum | solution.py:150
  (124 shorter events, 23.9 us)
Async XLA Ops:
  7.2 46.0 %copy-start = (bf16[768,2304]{1,0:T(8,128)(2,1)S(1)}, bf16[768,2304]{1,0:T(8,128)(2,1)}, u32[]{:S(2)}) copy-start(bf16[768,2304]{1,0:T(8,128)(2,1)} %param.19) | copy-start | bytes 10616836
  7.2 87.9 %all-gather.4.cloned.1.call-start = ((), (), s32[]{:S(2)}) async-start(), calls=%async_computation.1 | async-start | bytes 10027008 | tf_op jit(solution)/shard_map/all_gather | solution.py:120
  9.3 247.2 %reduce-scatter.2.cloned.1.call-start = ((), (), s32[]{:S(2)}) async-start(), calls=%async_computation.2 | async-start | bytes 10027008 | tf_op jit(solution)/shard_map/reduce_scatter | solution.py:149
  57.7 4.3 copy-start.25
  57.7 8.2 %copy-start.18 = (s32[512]{0:T(512)S(1)}, s32[512]{0:T(512)}, u32[]{:S(2)}) copy-start(s32[512]{0:T(512)} %param.32) | copy-start | bytes 6148
  66.1 3.5 copy-start.3
  69.7 4.6 copy-start.1
  73.4 5.6 %copy-start.13 = (f32[12,512]{1,0:T(8,128)}, f32[12,512]{1,0:T(8,128)S(1)}, u32[]{:S(2)}) copy-start(f32[12,512]{1,0:T(8,128)S(1)} %log_add_fusion) | copy-start | bytes 73732
  74.3 4.8 copy-start.24
  74.3 4.8 copy-start.29
  74.3 4.8 copy-start.31
  79.1 2.4 copy-start.12
  79.1 16.0 %copy-start.16 = (f32[3072]{0:T(1024)S(1)}, f32[3072]{0:T(1024)}, u32[]{:S(2)}) copy-start(f32[3072]{0:T(1024)} %convert_element_type.154) | copy-start | bytes 36868
  80.0 1.1 copy-start.6
  95.1 18.9 %copy-start.7 = (f32[512,768]{1,0:T(8,128)S(1)}, f32[512,768]{1,0:T(8,128)}, u32[]{:S(2)}) copy-start(f32[512,768]{1,0:T(8,128)} %copy-done.6) | copy-start | bytes 4718596
  95.1 18.9 %copy-start.19 = (f32[512]{0:T(512)S(1)}, f32[512]{0:T(512)}, u32[]{:S(2)}) copy-start(f32[512]{0:T(512)} %add_rsqrt_fusion.1) | copy-start | bytes 6148
  95.1 18.9 %copy-start.21 = (f32[768]{0:T(1024)S(1)}, f32[768]{0:T(1024)}, u32[]{:S(2)}) copy-start(f32[768]{0:T(1024)} %param.24) | copy-start | bytes 9220
  95.1 18.9 %copy-start.23 = (f32[768]{0:T(1024)S(1)}, f32[768]{0:T(1024)}, u32[]{:S(2)}) copy-start(f32[768]{0:T(1024)} %convert_element_type.157) | copy-start | bytes 9220
  95.1 18.9 %copy-start.28 = (bf16[2,3072,768]{2,1,0:T(8,128)(2,1)S(1)}, bf16[2,3072,768]{2,1,0:T(8,128)(2,1)}, u32[]{:S(2)}) copy-start(bf16[2,3072,768]{2,1,0:T(8,128)(2,1)} %all-gather.4.cloned.1.call-done) | copy-start | bytes 28311556
  95.1 18.9 %copy-start.32 = (f32[768]{0:T(1024)S(1)}, f32[768]{0:T(1024)}, u32[]{:S(2)}) copy-start(f32[768]{0:T(1024)} %param.25) | copy-start | bytes 9220
  114.1 3.1 copy-start.10
  114.1 3.1 copy-start.15
  114.1 4.4 copy-start.26
  121.2 4.4 copy-start.11
  121.2 4.4 copy-start.17
  131.9 1.7 copy-start.34
  146.8 0.7 copy-start.20
  146.8 0.7 copy-start.22
  146.8 166.9 %all-gather.6.cloned.1.call-start = ((), (), s32[]{:S(2)}) async-start(), calls=%async_computation.4 | async-start | bytes 1216512 | tf_op jit(solution)/shard_map/all_gather | solution.py:211
  147.5 8.3 %copy-start.8 = (f32[512,768]{1,0:T(8,128)S(1)}, f32[512,768]{1,0:T(8,128)}, u32[]{:S(2)}) copy-start(f32[512,768]{1,0:T(8,128)} %copy-done.6) | copy-start | bytes 4718596
  155.8 2.3 copy-start.30
  155.8 6.4 %copy-start.27 = (bf16[12]{0:T(256)(128)(2,1)S(1)}, bf16[12]{0:T(256)(128)(2,1)}, u32[]{:S(2)}) copy-start(bf16[12]{0:T(256)(128)(2,1)} %get-tuple-element.128) | copy-start | bytes 76
  156.9 1.1 copy-start.5
  162.1 14.9 %slice-start = ((s8[12582912]{0:T(1024)(128)(4,1)}), s8[4194304]{0:T(1024)(128)(4,1)S(1)}, s32[]{:S(2)}) async-start(s8[12582912]{0:T(1024)(128)(4,1)} %bitcast.107), calls=%async_computation.6 | async-start | bytes 8388608
  162.1 14.9 %slice-start.1 = ((s8[12582912]{0:T(1024)(128)(4,1)}), s8[4194304]{0:T(1024)(128)(4,1)S(1)}, s32[]{:S(2)}) async-start(s8[12582912]{0:T(1024)(128)(4,1)} %bitcast.107), calls=%async_computation.7 | async-start | bytes 8388608
  162.1 14.9 %slice-start.2 = ((s8[12582912]{0:T(1024)(128)(4,1)}), s8[4194304]{0:T(1024)(128)(4,1)S(1)}, s32[]{:S(2)}) async-start(s8[12582912]{0:T(1024)(128)(4,1)} %bitcast.107), calls=%async_computation.8 | async-start | bytes 8388608
  162.1 14.9 %copy-start.4 = (pred[512,512]{0,1:T(8,128)(4,1)S(1)}, pred[512,512]{0,1:T(8,128)(4,1)}, u32[]{:S(2)}) copy-start(pred[512,512]{0,1:T(8,128)(4,1)} %copy-done.3) | copy-start | bytes 786436
  162.2 14.9 %copy-start.14 = (f32[12,512]{1,0:T(8,128)S(1)}, f32[12,512]{1,0:T(8,128)}, u32[]{:S(2)}) copy-start(f32[12,512]{1,0:T(8,128)} %copy-done.13) | copy-start | bytes 73732
  177.0 7.8 %copy-start.2 = (bf16[512,2304]{0,1:T(8,128)(2,1)S(1)}, bf16[512,2304]{0,1:T(8,128)(2,1)}, u32[]{:S(2)}) copy-start(bf16[512,2304]{0,1:T(8,128)(2,1)} %copy.57) | copy-start | bytes 7077892
  186.8 1.1 copy-start.9
  205.9 258.0 %all-reduce.7.cloned.1.call-start = ((), (), s32[]{:S(2)}) async-start(), calls=%async_computation.5 | async-start | bytes 9437184 | tf_op jit(solution)/shard_map/psum | solution.py:195
  215.2 0.7 copy-start.33
  215.2 279.8 %all-reduce.5.cloned.1.call-start = ((), (), s32[]{:S(2)}) async-start(), calls=%async_computation.3 | async-start | bytes 1179648 | tf_op jit(solution)/shard_map/psum | solution.py:150
Sparse Core Ops, SparseCore 0:
  10.9 84.1 all-gather.3
  146.9 109.5 reduce-scatter.1
  260.0 53.6 all-gather.5
  320.0 143.9 all-reduce.6
  466.1 28.8 all-reduce.4
